TPU v7x, 512 devices: a whole 4x4x16 slice. The times are simulated.
512 devices in a mesh: row: 16 (over z_hi, y, core), col: 32 (over z_lo, x).
Axes of the slice: x: 4, y: 4, z: 16 (z_hi: 2, z_lo: 8; z = z_hi * 8 + z_lo), core: 2. Of those that a mesh axis runs over, the one named last changes fastest.
Arguments:
- query_grads: bfloat16 [256, 8192], P('row', 'col'), may hold values from -6 to 6
- query_acts: bfloat16 [256, 8192], P('col', 'row'), may hold values from -6 to 6
- train_grads: bfloat16 [512, 8192], P('row', 'col'), may hold values from -6 to 6
- train_acts: bfloat16 [512, 8192], P('col', 'row'), may hold values from -6 to 6
- grad_basis: bfloat16 [8192, 8192], P('col', 'row'), may hold values from -0.0625 to 0.0625
- act_basis: bfloat16 [8192, 8192], P('row', 'col'), may hold values from -0.0625 to 0.0625
- eigen_corr: float32 [8192, 8192], P('row', 'col'), may hold values from 0.02 to 2
- damping: float32 [], replicated, may hold values from 0.05 to 0.5
- query_seq: int32 [256], replicated, may hold values from 0 to 31, never falling along the last dimension, each value on 1 to 16 neighbouring positions
- train_doc: int32 [512], replicated, may hold values from 0 to 15, never falling along the last dimension, each value on 1 to 64 neighbouring positions
Outputs:
- scores: float32 [32, 512], P(None, 'col')
- doc_scores: float32 [32, 16], replicated
Inputs may be any that keep to these rules, and one draw needn't show every extreme that they name: `query_seq`: Non-decreasing along the query tokens; every sequence has 1 to 16 tokens, and one has exactly that many. `train_doc`: Non-decreasing along the training tokens; every document has 1 to 64 tokens, and one has exactly that many.
All inputs are finite; a program needn't handle non-finite values.
Results may differ from a plain program's by a relative error of at most 0.005.
Values may be sent and summed in bfloat16 or wider, within the bound.
No kernel may reach another device: no remote copies, remote signals or barrier semaphores. Data moves between devices by JAX's collectives and lax.ppermute only.
A program may use at most 64 MiB of HBM per device.

v0:
```python
import jax
import jax.numpy as jnp
from jax import lax
from jax.sharding import PartitionSpec as P

D = 8192
S = 32
DOCS = 16


def local(
    query_grads,
    query_acts,
    train_grads,
    train_acts,
    grad_basis,
    act_basis,
    eigen_corr,
    damping,
    query_seq,
    train_doc,
):
    grad_query, grad_train = (
        lax.all_gather(query_grads, "row", axis=0, tiled=True),
        lax.all_gather(train_grads, "row", axis=0, tiled=True),
    )
    act_query, act_train = (
        lax.all_gather(query_acts, "col", axis=0, tiled=True),
        lax.all_gather(train_acts, "col", axis=0, tiled=True),
    )
    grads_all = jnp.concatenate([grad_query, grad_train], axis=0)
    acts_all = jnp.concatenate([act_query, act_train], axis=0)
    n_query = grad_query.shape[0]
    grad_part = jnp.dot(grads_all, grad_basis, preferred_element_type=jnp.float32)
    grads_rot = lax.psum(grad_part, "col").astype(jnp.bfloat16)
    act_part = jnp.dot(acts_all, act_basis, preferred_element_type=jnp.float32)
    acts_rot = lax.psum(act_part, "row").astype(jnp.bfloat16)
    rot_gq = grads_rot[:n_query]
    rot_gu = grads_rot[n_query:]
    rot_aq = acts_rot[:n_query]
    rot_au = acts_rot[n_query:]
    denom = eigen_corr + damping
    act_wide = rot_au.astype(jnp.float32)
    row_block = eigen_corr.shape[0]
    col_block = eigen_corr.shape[1]
    group = 4

    def score_group(first):
        seq_ids = first + jnp.arange(group, dtype=jnp.int32)
        member = (query_seq[:, None] == seq_ids[None, :]).astype(jnp.bfloat16)
        weighted = (member[:, :, None] * rot_gq[:, None, :]).reshape(n_query, group * row_block)
        outer = lax.dot_general(
            weighted, rot_aq, (((0,), (0,)), ((), ())), preferred_element_type=jnp.float32
        )
        precond = (outer.reshape(group, row_block, col_block) / denom[None, :, :]).astype(
            jnp.bfloat16
        )
        mapped = jnp.einsum("ui,sij->usj", rot_gu, precond, preferred_element_type=jnp.float32)
        return jnp.sum(mapped * act_wide[:, None, :], axis=2).T

    starts = jnp.arange(S // group, dtype=jnp.int32) * group
    partial_scores = lax.map(score_group, starts).reshape(S, rot_gu.shape[0]) / D
    doc_table = (train_doc[:, None] == jnp.arange(DOCS, dtype=jnp.int32)[None, :]).astype(
        jnp.float32
    )
    counts = jnp.sum(doc_table, axis=0)
    owned = rot_gu.shape[0] // lax.axis_size("col")
    first_owned = lax.axis_index("col") * owned
    totals = lax.psum(partial_scores, ("row", "col"))
    scores = lax.dynamic_slice_in_dim(totals, first_owned, owned, 1)
    doc_sum = jnp.dot(totals, doc_table, precision=lax.Precision.HIGHEST)
    return (scores, doc_sum / counts[None, :])


def solution(mesh):
    in_specs = (
        P("row", "col"),
        P("col", "row"),
        P("row", "col"),
        P("col", "row"),
        P("col", "row"),
        P("row", "col"),
        P("row", "col"),
        P(),
        P(),
        P(),
    )
    out_specs = (P(None, "col"), P())
    return jax.shard_map(local, mesh=mesh, in_specs=in_specs, out_specs=out_specs, check_vma=False)
```

profile of v0, /device:TPU:1, one launch (start us, length us, event | category | flops | bytes accessed | tf_op | source)
XLA Modules:
  0.0 1171.2 jit_solution(7079369166472949300)
XLA Ops:
  7.2 52.0 %all_gather.13 = bf16[512,256]{1,0:T(8,128)(2,1)S(1)} all-gather(bf16[32,256]{1,0:T(8,128)(2,1)} %param.14), channel_id=1, replica_groups=mesh['row'=16,'col'=32] {'row'}, dimensions={0}, use_global_device_ids=true | all-gather | bytes 278528 | tf_op jit(solution)/shard_map/all_gather | solution.py:25
  59.2 34.3 %all_gather.12 = bf16[256,256]{1,0:T(8,128)(2,1)S(1)} all-gather(bf16[16,256]{1,0:T(8,128)(2,1)} %param.12), channel_id=1, replica_groups=mesh['row'=16,'col'=32] {'row'}, dimensions={0}, use_global_device_ids=true | all-gather | bytes 139264 | tf_op jit(solution)/shard_map/all_gather | solution.py:24
  93.5 0.4 fusion.16
  93.9 219.5 %all-reduce.5 = bf16[768,512]{1,0:T(8,128)(2,1)S(1)} all-reduce(f32[768,512]{1,0:T(8,128)S(1)} %fusion.16), channel_id=1, replica_groups=mesh['row'=16,'col'=32] {'col'}, use_global_device_ids=true, to_apply=%region_0.0 | all-reduce | flops 393216 | bytes 2359296 | tf_op jit(solution)/shard_map/psum | solution.py:35
  313.4 100.8 %all_gather.15 = bf16[512,512]{1,0:T(8,128)(2,1)S(1)} all-gather(bf16[16,512]{1,0:T(8,128)(2,1)S(1)} %copy-done.4), channel_id=1, replica_groups=mesh['row'=16,'col'=32] {'col'}, dimensions={0}, use_global_device_ids=true | all-gather | bytes 540672 | tf_op jit(solution)/shard_map/all_gather | solution.py:29
  414.2 100.0 %all_gather.14 = bf16[256,512]{1,0:T(8,128)(2,1)S(1)} all-gather(bf16[8,512]{1,0:T(8,128)(2,1)S(1)} %copy-done.5), channel_id=1, replica_groups=mesh['row'=16,'col'=32] {'col'}, dimensions={0}, use_global_device_ids=true | all-gather | bytes 270336 | tf_op jit(solution)/shard_map/all_gather | solution.py:28
  514.2 0.4 fusion.12
  514.6 176.3 %all-reduce.6 = bf16[768,256]{1,0:T(8,128)(2,1)S(1)} all-reduce(f32[768,256]{1,0:T(8,128)S(1)} %fusion.12), channel_id=1, replica_groups=mesh['row'=16,'col'=32] {'row'}, use_global_device_ids=true, to_apply=%region_1.0 | all-reduce | flops 196608 | bytes 1179648 | tf_op jit(solution)/shard_map/psum | solution.py:37
  691.0 0.1 copy.19
  691.1 0.2 copy.20
  692.1 19.3 %while.10 = (s32[]{:T(128)}, f32[8,4,512]{2,1,0:T(4,128)S(1)}, s32[256]{0:T(256)S(1)}, s32[8]{0:T(128)S(1)}, bf16[256,512]{0,1:T(8,128)(2,1)S(1)}, /*index=5*/bf...) while((s32[]{:T(128)}, f32[8,4,512]{2,1,0:T(4,128)S(1)}, ...), condition=%wide.region_4.5_spmd, body=%wide.region_2.4_spmd.sunk | while | flops 807927808 | bytes 1995929 | solution.py:62
  692.1 0.6 dynamic_slice.10
  692.7 0.6 iota_add_fusion.2
  693.3 0.1 compare_convert_fusion.2
  693.4 1.1 fusion.33
  694.5 0.6 dynamic_slice.10
  695.1 0.6 iota_add_fusion.2
  695.8 1.1 fusion.33
  696.9 0.6 dynamic_slice.10
  697.5 0.6 iota_add_fusion.2
  698.2 0.1 compare_convert_fusion.2
  698.2 1.1 fusion.33
  699.3 0.6 dynamic_slice.10
  699.9 0.6 iota_add_fusion.2
  700.6 0.1 compare_convert_fusion.2
  700.7 1.1 fusion.33
  701.8 0.6 dynamic_slice.10
  702.4 0.6 iota_add_fusion.2
  703.0 0.1 compare_convert_fusion.2
  703.1 1.1 fusion.33
  704.2 0.6 dynamic_slice.10
  704.8 0.6 iota_add_fusion.2
  705.4 0.1 compare_convert_fusion.2
  705.5 1.1 fusion.33
  706.6 0.6 dynamic_slice.10
  707.2 0.6 iota_add_fusion.2
  707.8 0.1 compare_convert_fusion.2
  707.9 1.1 fusion.33
  709.0 0.6 dynamic_slice.10
  709.6 0.6 iota_add_fusion.2
  710.3 0.1 compare_convert_fusion.2
  710.3 1.1 fusion.33
  711.5 0.6 div.26
  712.1 0.1 convert_reduce_fusion
  712.2 449.1 %all-reduce.4.cloned.1.call-done = f32[32,512]{1,0:T(8,128)} async-done(((f32[32,512]{1,0:T(8,128)}), f32[32,512]{1,0:T(8,128)}) %all-reduce.4.cloned.1.call-update) | async-done | bytes 65552 | tf_op jit(solution)/shard_map/psum | solution.py:69
  1161.3 0.8 constant_dynamic-slice_fusion
  1162.1 0.7 copy.21
  1162.8 1.6 convolution_divide_fusion
  (36 shorter events, 0.5 us)
Async XLA Ops:
  7.2 86.4 %copy-start = (bf16[256,512]{1,0:T(8,128)(2,1)S(1)}, bf16[256,512]{1,0:T(8,128)(2,1)}, u32[]{:S(2)}) copy-start(bf16[256,512]{1,0:T(8,128)(2,1)} %param.16) | copy-start | bytes 786436
  7.2 1154.2 %all-reduce.4.cloned.1.call-start = ((), (), s32[]{:S(2)}) async-start(), calls=%async_computation | async-start | bytes 131072 | tf_op jit(solution)/shard_map/psum | solution.py:69
  93.9 219.6 %copy-start.4 = (bf16[16,512]{1,0:T(8,128)(2,1)S(1)}, bf16[16,512]{1,0:T(8,128)(2,1)}, u32[]{:S(2)}) copy-start(bf16[16,512]{1,0:T(8,128)(2,1)} %param.15) | copy-start | bytes 49156
  313.4 201.2 %copy-start.1 = (bf16[768,512]{1,0:T(8,128)(2,1)}, bf16[768,512]{1,0:T(8,128)(2,1)S(1)}, u32[]{:S(2)}) copy-start(bf16[768,512]{1,0:T(8,128)(2,1)S(1)} %all-reduce.5) | copy-start | bytes 2359300
  313.4 100.8 %copy-start.5 = (bf16[8,512]{1,0:T(8,128)(2,1)S(1)}, bf16[8,512]{1,0:T(8,128)(2,1)}, u32[]{:S(2)}) copy-start(bf16[8,512]{1,0:T(8,128)(2,1)} %param.13) | copy-start | bytes 24580
  313.4 200.8 %copy-start.7 = (bf16[512,256]{1,0:T(8,128)(2,1)S(1)}, bf16[512,256]{1,0:T(8,128)(2,1)}, u32[]{:S(2)}) copy-start(bf16[512,256]{1,0:T(8,128)(2,1)} %param.17) | copy-start | bytes 786436
  690.9 1.1 copy-start.2
  690.9 1.2 slice-start
  690.9 1.2 copy-start.3
  692.1 20.0 %copy-start.6 = (s32[512]{0:T(512)S(1)}, s32[512]{0:T(512)}, u32[]{:S(2)}) copy-start(s32[512]{0:T(512)} %param.21) | copy-start | bytes 6148
Sparse Core Ops, SparseCore 0:
  712.2 449.0 all-reduce.3
where the time goes:
time: 1170 us
  blocking collectives  683 us (58%)
  waiting for transfers between devices  449 us (38%)
  between operations  14.9 us (1%)
    psum x1, waiting for transfers between devices, local(): totals = lax.psum(partial_scores, ('row', 'col'))  449 us
    psum x1, blocking collectives, local(): grads_rot = lax.psum(grad_part, 'col').astype(jnp.bfloat16)  219 us
    psum x1, blocking collectives, local(): acts_rot = lax.psum(act_part, 'row').astype(jnp.bfloat16)  176 us
    all_gather x1, blocking collectives, local(): lax.all_gather(train_acts, 'col', axis=0, tiled=True)  101 us
    all_gather x1, blocking collectives, local(): lax.all_gather(query_acts, 'col', axis=0, tiled=True)  100 us
    all_gather x1, blocking collectives, local(): lax.all_gather(train_grads, 'row', axis=0, tiled=True)  52 us
    all_gather x1, blocking collectives, local(): lax.all_gather(query_grads, 'row', axis=0, tiled=True)  34.3 us
  transfers between devices with their start and end apart: 1, of which 1 were waited for; matrix products, arithmetic and copies ran while one was open for 0% of the time, Pallas kernels for 0%

commit v1 on v0

--- a/solution.py
+++ b/solution.py
@@ -32,7 +32,7 @@
     acts_all = jnp.concatenate([act_query, act_train], axis=0)
     n_query = grad_query.shape[0]
     grad_part = jnp.dot(grads_all, grad_basis, preferred_element_type=jnp.float32)
-    grads_rot = lax.psum(grad_part, "col").astype(jnp.bfloat16)
+    grads_rot = jnp.sum(lax.all_gather(grad_part, "col"), axis=0).astype(jnp.bfloat16)
     act_part = jnp.dot(acts_all, act_basis, preferred_element_type=jnp.float32)
     acts_rot = lax.psum(act_part, "row").astype(jnp.bfloat16)
     rot_gq = grads_rot[:n_query]

time: 1170 us -> 1260 us (1.077)
  waiting for transfers between devices: 449 us -> 732 us
  blocking collectives: 683 us -> 467 us
  other arithmetic: 5.97 us -> 23.9 us
    psum x1 -> x0, blocking collectives: 219 us -> none  [local(): grads_rot = lax.psum(grad_part, 'col').astype(jnp.bfloat16)]
    all_gather x0 -> x1, waiting for transfers between devices: none -> 180 us  [local(): lax.all_gather(grad_part, 'col')]
    psum x1, waiting for transfers between devices: 449 us -> 552 us  [local(): totals = lax.psum(partial_scores, ('row', 'col'))]
    psum x1, blocking collectives: 176 us -> 152 us  [local(): acts_rot = lax.psum(act_part, 'row').astype(jnp.bfloat16)]
    reduce_sum x0 -> x1, other arithmetic: none -> 18 us  [local(): jnp.sum(lax.all_gather(grad_part, 'col'), axis=0).astype(jnp.bfloat16)]
    all_gather x1, blocking collectives: 100 us -> 114 us  [local(): lax.all_gather(query_acts, 'col', axis=0, tiled=True)]
    all_gather x1, blocking collectives: 101 us -> 114 us  [local(): lax.all_gather(train_acts, 'col', axis=0, tiled=True)]
  transfers between devices with their start and end apart: 1 -> 2, of which waited for: 1 -> 2; matrix products, arithmetic and copies ran while one was open for 0% -> 0% of each run, Pallas kernels for 0% -> 0%
where the time goes in v1:
time: 1260 us
  waiting for transfers between devices  732 us (58%)
  blocking collectives  467 us (37%)
  other arithmetic  23.9 us (2%)
  between operations  14.9 us (1%)
    psum x1, waiting for transfers between devices, local(): totals = lax.psum(partial_scores, ('row', 'col'))  552 us
    all_gather x1, waiting for transfers between devices, local(): lax.all_gather(grad_part, 'col')  180 us
    psum x1, blocking collectives, local(): acts_rot = lax.psum(act_part, 'row').astype(jnp.bfloat16)  152 us
    all_gather x1, blocking collectives, local(): lax.all_gather(train_acts, 'col', axis=0, tiled=True)  114 us
    all_gather x1, blocking collectives, local(): lax.all_gather(query_acts, 'col', axis=0, tiled=True)  114 us
    all_gather x1, blocking collectives, local(): lax.all_gather(train_grads, 'row', axis=0, tiled=True)  52 us
    all_gather x1, blocking collectives, local(): lax.all_gather(query_grads, 'row', axis=0, tiled=True)  34.4 us
  transfers between devices with their start and end apart: 2, of which 2 were waited for; matrix products, arithmetic and copies ran while one was open for 0% of the time, Pallas kernels for 0%

profile of v1, /device:TPU:1, one launch (start us, length us, event | category | flops | bytes accessed | tf_op | source)
XLA Modules:
  0.0 1257.2 jit_solution(4493111985102150418)
XLA Ops:
  7.2 52.0 %all_gather.19 = bf16[512,256]{1,0:T(8,128)(2,1)S(1)} all-gather(bf16[32,256]{1,0:T(8,128)(2,1)} %param.14), channel_id=1, replica_groups=mesh['row'=16,'col'=32] {'row'}, dimensions={0}, use_global_device_ids=true | all-gather | bytes 278528 | tf_op jit(solution)/shard_map/all_gather | solution.py:25
  59.3 34.4 %all_gather.18 = bf16[256,256]{1,0:T(8,128)(2,1)S(1)} all-gather(bf16[16,256]{1,0:T(8,128)(2,1)} %param.12), channel_id=1, replica_groups=mesh['row'=16,'col'=32] {'row'}, dimensions={0}, use_global_device_ids=true | all-gather | bytes 139264 | tf_op jit(solution)/shard_map/all_gather | solution.py:24
  93.7 1.5 fusion.16
  95.3 114.2 %all_gather.22 = bf16[256,512]{1,0:T(8,128)(2,1)S(1)} all-gather(bf16[8,512]{1,0:T(8,128)(2,1)S(1)} %copy-done.4), channel_id=1, replica_groups=mesh['row'=16,'col'=32] {'col'}, dimensions={0}, use_global_device_ids=true | all-gather | bytes 270336 | tf_op jit(solution)/shard_map/all_gather | solution.py:28
  209.5 114.3 %all_gather.23 = bf16[512,512]{1,0:T(8,128)(2,1)S(1)} all-gather(bf16[16,512]{1,0:T(8,128)(2,1)S(1)} %copy-done.3), channel_id=1, replica_groups=mesh['row'=16,'col'=32] {'col'}, dimensions={0}, use_global_device_ids=true | all-gather | bytes 540672 | tf_op jit(solution)/shard_map/all_gather | solution.py:29
  323.7 0.4 fusion.12
  324.1 151.8 %all-reduce.4 = bf16[768,256]{1,0:T(8,128)(2,1)S(1)} all-reduce(f32[768,256]{1,0:T(8,128)S(1)} %fusion.12), channel_id=1, replica_groups=mesh['row'=16,'col'=32] {'row'}, use_global_device_ids=true, to_apply=%region_1.0 | all-reduce | flops 196608 | bytes 1179648 | tf_op jit(solution)/shard_map/psum | solution.py:37
  476.6 0.2 copy.20
  476.9 180.1 %all-gather.3.cloned.1.call-done = f32[24576,512]{1,0:T(8,128)} async-done(((f32[768,512]{1,0:T(8,128)}), f32[24576,512]{1,0:T(8,128)}) %all-gather.3.cloned.1.call-update) | async-done | bytes 50331664 | tf_op jit(solution)/shard_map/all_gather | solution.py:35
  657.0 18.0 %reduce_sum.27 = bf16[768,512]{1,0:T(8,128)(2,1)S(1)} reduce(f32[32,768,512]{2,1,0:T(8,128)} %bitcast.41, f32[]{:T(128)} %constant.3.clone.1), dimensions={0}, to_apply=%region_0.0 | reduce | flops 12189696 | bytes 51118084 | tf_op jit(solution)/shard_map/reduce_sum | solution.py:35
  675.1 0.1 copy.19
  675.2 0.5 copy-done.2
  675.7 19.3 %while.10 = (s32[]{:T(128)}, f32[8,4,512]{2,1,0:T(4,128)S(1)}, s32[256]{0:T(256)S(1)}, s32[8]{0:T(128)S(1)}, bf16[256,512]{0,1:T(8,128)(2,1)S(1)}, /*index=5*/bf...) while((s32[]{:T(128)}, f32[8,4,512]{2,1,0:T(4,128)S(1)}, ...), condition=%wide.region_4.5_spmd, body=%wide.region_2.4_spmd.sunk | while | flops 807927808 | bytes 1995937 | solution.py:62
  675.7 0.6 dynamic_slice.10
  676.2 0.6 iota_add_fusion.2
  676.9 0.1 compare_convert_fusion.2
  677.0 1.1 fusion.33
  678.1 0.6 dynamic_slice.10
  678.6 0.6 iota_add_fusion.2
  679.3 0.1 compare_convert_fusion.2
  679.4 1.1 fusion.33
  680.5 0.6 dynamic_slice.10
  681.1 0.6 iota_add_fusion.2
  681.7 0.1 compare_convert_fusion.2
  681.8 1.1 fusion.33
  682.9 0.6 dynamic_slice.10
  683.5 0.6 iota_add_fusion.2
  684.1 0.1 compare_convert_fusion.2
  684.2 1.1 fusion.33
  685.3 0.6 dynamic_slice.10
  685.9 0.6 iota_add_fusion.2
  686.6 0.1 compare_convert_fusion.2
  686.6 1.1 fusion.33
  687.7 0.6 dynamic_slice.10
  688.3 0.6 iota_add_fusion.2
  689.0 1.1 fusion.33
  690.1 0.6 dynamic_slice.10
  690.7 0.6 iota_add_fusion.2
  691.5 1.1 fusion.33
  692.6 0.6 dynamic_slice.10
  693.1 0.6 iota_add_fusion.2
  693.9 1.1 fusion.33
  695.0 0.6 div.26
  695.7 0.1 convert_reduce_fusion
  695.8 551.5 %all-reduce.3.cloned.1.call-done = f32[32,512]{1,0:T(8,128)} async-done(((f32[32,512]{1,0:T(8,128)}), f32[32,512]{1,0:T(8,128)}) %all-reduce.3.cloned.1.call-update) | async-done | bytes 65552 | tf_op jit(solution)/shard_map/psum | solution.py:69
  1247.3 0.8 constant_dynamic-slice_fusion
  1248.1 0.7 copy.21
  1248.8 1.6 convolution_divide_fusion
  (36 shorter events, 0.6 us)
Async XLA Ops:
  7.2 86.5 %copy-start = (bf16[256,512]{1,0:T(8,128)(2,1)S(1)}, bf16[256,512]{1,0:T(8,128)(2,1)}, u32[]{:S(2)}) copy-start(bf16[256,512]{1,0:T(8,128)(2,1)} %param.16) | copy-start | bytes 786436
  7.2 88.1 %copy-start.4 = (bf16[8,512]{1,0:T(8,128)(2,1)S(1)}, bf16[8,512]{1,0:T(8,128)(2,1)}, u32[]{:S(2)}) copy-start(bf16[8,512]{1,0:T(8,128)(2,1)} %param.13) | copy-start | bytes 24580
  7.2 649.8 %all-gather.3.cloned.1.call-start = ((), (), s32[]{:S(2)}) async-start(), calls=%async_computation.1 | async-start | bytes 51904512 | tf_op jit(solution)/shard_map/all_gather | solution.py:35
  59.3 150.2 %copy-start.3 = (bf16[16,512]{1,0:T(8,128)(2,1)S(1)}, bf16[16,512]{1,0:T(8,128)(2,1)}, u32[]{:S(2)}) copy-start(bf16[16,512]{1,0:T(8,128)(2,1)} %param.15) | copy-start | bytes 49156
  93.7 230.1 %copy-start.6 = (bf16[512,256]{1,0:T(8,128)(2,1)S(1)}, bf16[512,256]{1,0:T(8,128)(2,1)}, u32[]{:S(2)}) copy-start(bf16[512,256]{1,0:T(8,128)(2,1)} %param.17) | copy-start | bytes 786436
  95.2 1152.1 %all-reduce.3.cloned.1.call-start = ((), (), s32[]{:S(2)}) async-start(), calls=%async_computation | async-start | bytes 131072 | tf_op jit(solution)/shard_map/psum | solution.py:69
  324.1 152.8 %copy-start.1 = (f32[512,256]{1,0:T(8,128)S(1)}, f32[512,256]{1,0:T(8,128)}, u32[]{:S(2)}) copy-start(f32[512,256]{1,0:T(8,128)} %param.18) | copy-start | bytes 1572868
  675.0 0.7 copy-start.2
  675.7 20.0 %copy-start.5 = (s32[512]{0:T(512)S(1)}, s32[512]{0:T(512)}, u32[]{:S(2)}) copy-start(s32[512]{0:T(512)} %param.21) | copy-start | bytes 6148
Sparse Core Ops, SparseCore 0:
  95.3 561.6 all-gather.2
  695.8 551.4 all-reduce.2
